TPU v7x, 32 devices: a whole 2x2x4 slice. The times are simulated.
32 devices in a mesh: ctx: 4 (over y, x), wsh: 8 (over z, core).
Axes of the slice: x: 2, y: 2, z: 4, core: 2. Of those that a mesh axis runs over, the one named last changes fastest.
Arguments:
- tokens: bfloat16 [8, 2048, 768], P('wsh', 'ctx'), may hold values from -6 to 6
- cluster_order: int32 [8, 2048], P('wsh', 'ctx'), may hold values from 0 to 2047, as said below
- qkv_weight: bfloat16 [768, 2304], P('wsh'), may hold values from -0.21875 to 0.21875
- query_bias: bfloat16 [768], P('wsh'), may hold values from -3 to 3
- value_bias: bfloat16 [768], P('wsh'), may hold values from -1.25 to 1.25
- out_weight: bfloat16 [768, 768], P('wsh'), may hold values from -1.25 to 1.25
- out_bias: bfloat16 [768], P('wsh'), may hold values from -1.75 to 1.75
- first_gain: bfloat16 [768], P('wsh'), may hold values from 0.25 to 1.75
- first_shift: bfloat16 [768], P('wsh'), may hold values from -1.75 to 1.75
- up_weight: bfloat16 [768, 3072], P('wsh'), may hold values from -0.21875 to 0.21875
- up_bias: bfloat16 [3072], P('wsh'), may hold values from -3 to 3
- down_weight: bfloat16 [3072, 768], P('wsh'), may hold values from -0.109375 to 0.109375
- down_bias: bfloat16 [768], P('wsh'), may hold values from -1.75 to 1.75
- second_gain: bfloat16 [768], P('wsh'), may hold values from 0.25 to 1.75
- second_shift: bfloat16 [768], P('wsh'), may hold values from -1.75 to 1.75
- cotangent: bfloat16 [8, 2048, 768], P('wsh', 'ctx'), may hold values from -6 to 6
Outputs:
- layer_out: bfloat16 [8, 2048, 768], P('wsh', 'ctx')
- grad_tokens: float32 [8, 2048, 768], P('wsh', 'ctx')
- grad_qkv_weight: float32 [768, 2304], P('wsh')
- grad_query_bias: float32 [768], P('wsh')
- grad_value_bias: float32 [768], P('wsh')
- grad_out_weight: float32 [768, 768], P('wsh')
- grad_out_bias: float32 [768], P('wsh')
- grad_first_gain: float32 [768], P('wsh')
- grad_first_shift: float32 [768], P('wsh')
- grad_up_weight: float32 [768, 3072], P('wsh')
- grad_up_bias: float32 [3072], P('wsh')
- grad_down_weight: float32 [3072, 768], P('wsh')
- grad_down_bias: float32 [768], P('wsh')
- grad_second_gain: float32 [768], P('wsh')
- grad_second_shift: float32 [768], P('wsh')
Inputs may be any that keep to these rules, and one draw needn't show every extreme that they name: `cluster_order`: each stream's row is a permutation of its positions. The stream is cut into four documents, each a multiple of 128 tokens long, the longest exactly 1024; the permutation maps every document's positions onto themselves, so each cluster lies within one document.
All inputs are finite; a program needn't handle non-finite values.
Results may differ from a plain program's by a relative error of at most 0.02.
Values may be sent and summed in bfloat16 or wider, within the bound.
A program may use at most 128 MiB of HBM per device.

v0:
```python
import jax
import jax.numpy as jnp
from jax import lax
from jax.sharding import PartitionSpec as P

HEAD_DIM = 64
CLUSTER = 128
epsilon = 1e-05


def inner(left, right):
    return lax.dot_general(
        left, right, (((0,), (0,)), ((), ())), preferred_element_type=jnp.float32
    )


def times_transposed(left, right):
    return lax.dot_general(
        left, right, (((1,), (1,)), ((), ())), preferred_element_type=jnp.float32
    )


def normalize(values):
    centre = values - jnp.mean(values, axis=1, keepdims=True)
    factor = lax.rsqrt(jnp.mean(centre * centre, axis=1, keepdims=True) + epsilon)
    return (centre * factor, factor)


def norm_back(grad_out, normed, factor, gain):
    grad_normed = grad_out * gain
    return factor * (
        grad_normed
        - jnp.mean(grad_normed, axis=1, keepdims=True)
        - normed * jnp.mean(grad_normed * normed, axis=1, keepdims=True)
    )


def on_device(
    tokens,
    cluster_order,
    qkv_weight,
    query_bias,
    value_bias,
    out_weight,
    out_bias,
    first_gain,
    first_shift,
    up_weight,
    up_bias,
    down_weight,
    down_bias,
    second_gain,
    second_shift,
    cotangent,
):
    order = cluster_order[0]
    rows = tokens.shape[1]
    width = tokens.shape[2]
    heads = width // HEAD_DIM
    blocks = rows // CLUSTER
    group_rows = rows * lax.axis_size("ctx")
    first_row = lax.axis_index("ctx") * rows
    factor_qk = HEAD_DIM ** (-0.5)
    small = [
        query_bias,
        value_bias,
        out_bias,
        first_gain,
        first_shift,
        down_bias,
        second_gain,
        second_shift,
        up_bias,
    ]
    sizes = [v.shape[0] for v in small]
    packed = lax.all_gather(jnp.concatenate(small), "wsh", axis=0, tiled=False)
    spots = [sum(sizes[:i]) for i in range(len(sizes))]
    qbias, vbias, obias, gain_one, shift_one, dbias, gain_two, shift_two, ubias = [
        packed[:, s : s + n].reshape(-1).astype(jnp.float32) for s, n in zip(spots, sizes)
    ]
    whole_order = lax.all_gather(order, "ctx", axis=0, tiled=True)
    both = lax.all_gather(
        jnp.concatenate([tokens[0], cotangent[0]], axis=1), "ctx", axis=0, tiled=True
    )
    whole_qkv = lax.all_gather(qkv_weight, "wsh", axis=0, tiled=True)
    whole_out = lax.all_gather(out_weight, "wsh", axis=0, tiled=True)
    whole_up = lax.all_gather(up_weight, "wsh", axis=0, tiled=True)
    whole_down = lax.all_gather(down_weight, "wsh", axis=0, tiled=True)
    take = (order[:, None] == jnp.arange(group_rows, dtype=jnp.int32)[None, :]).astype(jnp.bfloat16)
    home = (
        (first_row + jnp.arange(rows, dtype=jnp.int32))[:, None] == whole_order[None, :]
    ).astype(jnp.bfloat16)
    mine = jnp.dot(take, both, preferred_element_type=jnp.float32)
    inputs = mine[:, :width].astype(jnp.bfloat16)
    grad_top = mine[:, width:]
    qkv_shift = jnp.concatenate([qbias, jnp.zeros((width,), jnp.float32), vbias])
    own_qkv = (jnp.dot(inputs, whole_qkv, preferred_element_type=jnp.float32) + qkv_shift).astype(
        jnp.bfloat16
    )
    query = own_qkv[:, :width].reshape(blocks, CLUSTER, heads, HEAD_DIM)
    keyed = own_qkv[:, width : 2 * width].reshape(blocks, CLUSTER, heads, HEAD_DIM)
    valued = own_qkv[:, 2 * width :].reshape(blocks, CLUSTER, heads, HEAD_DIM)
    places = order.reshape(blocks, CLUSTER)
    visible = (places[:, None, :] <= places[:, :, None])[:, None, :, :]
    scores = (
        jnp.einsum("cihd,cjhd->chij", query, keyed, preferred_element_type=jnp.float32) * factor_qk
    )
    masked = jnp.where(visible, scores, -1e30)
    row_max = jnp.max(masked, axis=3, keepdims=True)
    expd = jnp.where(visible, jnp.exp(masked - row_max), 0.0)
    total = jnp.sum(expd, axis=3, keepdims=True)
    probs_full = expd / total
    probs = probs_full.astype(jnp.bfloat16)
    context = (
        jnp.einsum("chij,cjhd->cihd", probs, valued, preferred_element_type=jnp.float32)
        .astype(jnp.bfloat16)
        .reshape(rows, width)
    )
    attended = (
        (jnp.dot(context, whole_out, preferred_element_type=jnp.float32) + obias)
        .astype(jnp.bfloat16)
        .astype(jnp.float32)
    )
    resid = inputs.astype(jnp.float32) + attended
    first_norm, first_factor = normalize(resid)
    first_out = first_norm * gain_one + shift_one
    first_low = first_out.astype(jnp.bfloat16)
    pre_act = jnp.dot(first_low, whole_up, preferred_element_type=jnp.float32) + ubias
    half = 0.5 * (1.0 + lax.erf(pre_act * 0.7071067811865476))
    hidden = (pre_act * half).astype(jnp.bfloat16)
    slope = half + pre_act * jnp.exp(-0.5 * pre_act * pre_act) * 0.3989422804014327
    second_in = first_out + jnp.dot(hidden, whole_down, preferred_element_type=jnp.float32) + dbias
    second_norm, second_factor = normalize(second_in)
    layer_out = (second_norm * gain_two + shift_two).astype(jnp.bfloat16)
    group_out = lax.all_gather(layer_out, "ctx", axis=0, tiled=True)
    out_home = jnp.dot(home, group_out, preferred_element_type=jnp.float32).astype(jnp.bfloat16)
    grad_gain_two = jnp.sum(grad_top * second_norm, axis=0)
    grad_shift_two = jnp.sum(grad_top, axis=0)
    grad_second = norm_back(grad_top, second_norm, second_factor, gain_two)
    grad_branch2 = grad_second.astype(jnp.bfloat16)
    grad_down_w = inner(hidden, grad_branch2).astype(jnp.bfloat16)
    grad_down_b = jnp.sum(grad_branch2.astype(jnp.float32), axis=0)
    grad_hidden = times_transposed(grad_branch2, whole_down)
    grad_pre = (grad_hidden * slope).astype(jnp.bfloat16)
    grad_up_w = inner(first_low, grad_pre).astype(jnp.bfloat16)
    grad_up_b = jnp.sum(grad_pre.astype(jnp.float32), axis=0)
    grad_first = grad_second + times_transposed(grad_pre, whole_up)
    grad_gain_one = jnp.sum(grad_first * first_norm, axis=0)
    grad_shift_one = jnp.sum(grad_first, axis=0)
    grad_resid = norm_back(grad_first, first_norm, first_factor, gain_one)
    grad_attended = grad_resid.astype(jnp.bfloat16)
    grad_out_b = jnp.sum(grad_attended.astype(jnp.float32), axis=0)
    grad_out_w = inner(context, grad_attended).astype(jnp.bfloat16)
    grad_context = (
        times_transposed(grad_attended, whole_out)
        .astype(jnp.bfloat16)
        .reshape(blocks, CLUSTER, heads, HEAD_DIM)
    )
    grad_probs = jnp.einsum(
        "cihd,cjhd->chij", grad_context, valued, preferred_element_type=jnp.float32
    )
    grad_valued = jnp.einsum(
        "chij,cihd->cjhd", probs, grad_context, preferred_element_type=jnp.float32
    ).astype(jnp.bfloat16)
    inner_sum = jnp.sum(probs_full * grad_probs, axis=3, keepdims=True)
    grad_scores = (probs_full * (grad_probs - inner_sum)).astype(jnp.bfloat16)
    grad_query = (
        jnp.einsum("chij,cjhd->cihd", grad_scores, keyed, preferred_element_type=jnp.float32)
        * factor_qk
    ).astype(jnp.bfloat16)
    grad_keyed = (
        jnp.einsum("chij,cihd->cjhd", grad_scores, query, preferred_element_type=jnp.float32)
        * factor_qk
    ).astype(jnp.bfloat16)
    own_grad = jnp.concatenate(
        [
            grad_query.reshape(rows, width),
            grad_keyed.reshape(rows, width),
            grad_valued.reshape(rows, width),
        ],
        axis=1,
    )
    grad_query_b = jnp.sum(own_grad[:, :width].astype(jnp.float32), axis=0)
    grad_value_b = jnp.sum(own_grad[:, 2 * width :].astype(jnp.float32), axis=0)
    grad_qkv_w = inner(inputs, own_grad).astype(jnp.bfloat16)
    grad_inputs = (grad_resid + times_transposed(own_grad, whole_qkv)).astype(jnp.bfloat16)
    group_in = lax.all_gather(grad_inputs, "ctx", axis=0, tiled=True)
    in_home = jnp.dot(home, group_in, preferred_element_type=jnp.float32)

    def summed(grad):
        part = lax.psum_scatter(grad, "wsh", scatter_dimension=0, tiled=True)
        return lax.psum(part, "ctx").astype(jnp.float32)

    sums = [summed(g) for g in (grad_down_w, grad_up_w, grad_out_w, grad_qkv_w)]
    small_grads = [
        grad_query_b,
        grad_value_b,
        grad_out_b,
        grad_gain_one,
        grad_shift_one,
        grad_down_b,
        grad_gain_two,
        grad_shift_two,
        grad_up_b,
    ]
    parts = lax.axis_size("wsh")
    table = jnp.concatenate([g.reshape(parts, -1) for g in small_grads], axis=1)
    table = lax.psum(table, ("ctx", "wsh"))
    own = lax.dynamic_slice_in_dim(table, lax.axis_index("wsh"), 1, 0)[0]
    g_q, g_v, g_o, g_g1, g_s1, g_d, g_g2, g_s2, g_u = [own[s : s + n] for s, n in zip(spots, sizes)]
    return (
        out_home[None],
        in_home[None],
        sums[3],
        g_q,
        g_v,
        sums[2],
        g_o,
        g_g1,
        g_s1,
        sums[1],
        g_u,
        sums[0],
        g_d,
        g_g2,
        g_s2,
    )


def solution(mesh):
    row = P("wsh", None)
    vec = P("wsh")
    seq = P("wsh", "ctx", None)
    in_specs = (
        seq,
        P("wsh", "ctx"),
        row,
        vec,
        vec,
        row,
        vec,
        vec,
        vec,
        row,
        vec,
        row,
        vec,
        vec,
        vec,
        seq,
    )
    out_specs = (seq, seq, row, vec, vec, row, vec, vec, vec, row, vec, row, vec, vec, vec)
    return jax.shard_map(
        on_device, mesh=mesh, in_specs=in_specs, out_specs=out_specs, check_vma=False
    )
```

profile of v0, /device:TPU:0, one launch (start us, length us, event | category | flops | bytes accessed | tf_op | source)
XLA Modules:
  0.0 654.2 jit_solution(16202312041115670555)
XLA Ops:
  7.2 2.6 pad_maximum_fusion
  12.8 15.7 %all-gather.2 = bf16[8,1,1152]{2,1,0:T(2,128)(2,1)S(1)} all-gather(bf16[1,1,1152]{2,1,0:T(2,128)(2,1)S(1)} %reshape.237), channel_id=3, replica_groups=mesh['ctx'=4,'wsh'=8] {'wsh'}, dimensions={0}, use_global_device_ids=true | all-gather | bytes 20736 | tf_op jit(solution)/shard_map/all_gather | solution.py:76
  29.4 53.9 %all-gather.11.cloned.1.call-done = bf16[2048,1536]{1,0:T(8,128)(2,1)} async-done(((bf16[512,1536]{1,0:T(8,128)(2,1)}), bf16[2048,1536]{1,0:T(8,128)(2,1)}) %all-gather.11.cloned.1.call-update) | async-done | bytes 6291472 | tf_op jit(solution)/shard_map/all_gather | solution.py:82
  83.3 5.8 fusion.12
  89.2 37.4 %all-gather.13.cloned.1.call-done = bf16[768,2304]{1,0:T(8,128)(2,1)} async-done(((bf16[96,2304]{1,0:T(8,128)(2,1)}), bf16[768,2304]{1,0:T(8,128)(2,1)}) %all-gather.13.cloned.1.call-update) | async-done | bytes 3538960 | tf_op jit(solution)/shard_map/all_gather | solution.py:85
  126.5 4.0 fusion.11
  130.5 1.4 fusion.67
  132.0 1.5 copy.64
  135.7 1.0 fusion.68
  137.4 1.0 copy-done.11
  139.0 10.7 %all-gather.15.cloned.1.call-done = bf16[768,768]{1,0:T(8,128)(2,1)} async-done(((bf16[96,768]{1,0:T(8,128)(2,1)}), bf16[768,768]{1,0:T(8,128)(2,1)}) %all-gather.15.cloned.1.call-update) | async-done | bytes 1179664 | tf_op jit(solution)/shard_map/all_gather | solution.py:86
  149.7 2.7 fusion.26
  152.4 2.1 multiply_reduce_fusion.6
  154.5 48.2 %all-gather.17.cloned.1.call-done = bf16[768,3072]{1,0:T(8,128)(2,1)} async-done(((bf16[96,3072]{1,0:T(8,128)(2,1)}), bf16[768,3072]{1,0:T(8,128)(2,1)}) %all-gather.17.cloned.1.call-update) | async-done | bytes 4718608 | tf_op jit(solution)/shard_map/all_gather | solution.py:87
  202.7 9.0 %multiply_convert_fusion = (bf16[512,3072]{1,0:T(8,128)(2,1)}, f32[512,3072]{1,0:T(8,128)}) fusion(f32[3072]{0:T(1024)S(1)} %reshape.231, bf16[768,3072]{1,0:T(8,128)(2,1)} %all-gather.17.cloned.1.call-done, f32[768]{0:T(1024)S(1)} %reshape.230, f32[768]{0:T(1024)S(1)} %reshape.229, f32[512]{0:T(512)S(1)} %add_rsqrt_fusion.1, ...), kind=kOutput, calls=%fused_computation.9 | convolution fusion | flops 2428502016 | bytes 15751168 | tf_op jit(solution)/shard_map/dot_general | solution.py:128
  211.8 43.0 %all-gather.19.cloned.1.call-done = bf16[3072,768]{1,0:T(8,128)(2,1)} async-done(((bf16[384,768]{1,0:T(8,128)(2,1)}), bf16[3072,768]{1,0:T(8,128)(2,1)}) %all-gather.19.cloned.1.call-update) | async-done | bytes 4718608 | tf_op jit(solution)/shard_map/all_gather | solution.py:88
  254.8 6.7 %fusion.69 = (f32[512]{0:T(512)S(1)}, f32[512,768]{1,0:T(8,128)S(1)}) fusion(f32[768]{0:T(1024)S(1)} %reshape.232, bf16[512,3072]{1,0:T(8,128)(2,1)} %get-tuple-element.55, bf16[3072,768]{1,0:T(8,128)(2,1)} %all-gather.19.cloned.1.call-done, f32[768]{0:T(1024)S(1)} %reshape.230, f32[768]{0:T(1024)S(1)} %reshape.229, f32[512]{0:T(512)S(1)} %add_rsqrt_fusion.1, ...), kind=kOutput, calls=%fused_computation.137 | convolution fusion | flops 2419850752 | bytes 11025408 | tf_op jit(solution)/shard_map/dot_general | solution.py:132
  262.7 1.5 convert_reduce_fusion.1
  264.2 4.7 convert_reduce_fusion
  269.0 3.2 multiply_reduce_fusion.2
  272.3 1.9 convert_reduce_fusion.2
  274.1 1.7 convolution_convert_fusion.4
  275.9 2.3 copy.71
  278.2 2.6 reshape.213
  280.8 4.4 convert_reduce_fusion.3
  285.2 2.5 multiply_reduce_fusion
  287.7 1.8 convolution_convert_fusion.3
  289.5 2.6 copy.82
  292.2 3.8 multiply_convert_fusion.1
  295.9 1.2 fusion.38
  299.7 1.4 copy-done.19
  301.8 3.9 convolution_convert_fusion.2
  305.8 7.2 %convolution_convert_fusion.1 = bf16[768,3072]{1,0:T(8,128)(2,1)} fusion(bf16[512,3072]{1,0:T(8,128)(2,1)} %copy-done.34, f32[768]{0:T(1024)S(1)} %reshape.230, f32[768]{0:T(1024)S(1)} %reshape.229, bf16[512,768]{1,0:T(8,128)(2,1)} %copy-done.5, f32[512]{0:T(512)S(1)} %add_rsqrt_fusion.1, f32[512]{0:T(512)S(1)} %broadcast_multiply_fusion.5, ...), kind=kOutput, calls=%fused_computation.16 | convolution fusion | flops 2421424128 | bytes 9449472 | tf_op jit(solution)/shard_map/dot_general | solution.py:12
  313.2 1.1 copy-done.14
  314.3 6.7 %convolution_convert_fusion = bf16[3072,768]{1,0:T(8,128)(2,1)} fusion(bf16[512,3072]{1,0:T(8,128)(2,1)} %get-tuple-element.55, f32[512,768]{1,0:T(8,128)S(1)} %copy-done.14), kind=kOutput, calls=%fused_computation.15 | convolution fusion | flops 2418671616 | bytes 9437184 | tf_op jit(solution)/shard_map/dot_general | solution.py:12
  321.1 1.3 copy-done.4
  322.5 5.7 add_convert_fusion
  329.0 39.3 %reduce-scatter.5.cloned.1.call-done = bf16[96,2304]{1,0:T(8,128)(2,1)} async-done(((bf16[768,2304]{1,0:T(8,128)(2,1)}), bf16[96,2304]{1,0:T(8,128)(2,1)}) %reduce-scatter.5.cloned.1.call-update) | async-done | bytes 442384 | tf_op jit(solution)/shard_map/reduce_scatter | solution.py:191
  368.3 55.9 %reduce-scatter.9.cloned.1.call-done = bf16[96,3072]{1,0:T(8,128)(2,1)} async-done(((bf16[768,3072]{1,0:T(8,128)(2,1)}), bf16[96,3072]{1,0:T(8,128)(2,1)}) %reduce-scatter.9.cloned.1.call-update) | async-done | bytes 589840 | tf_op jit(solution)/shard_map/reduce_scatter | solution.py:191
  424.2 55.8 %reduce-scatter.11.cloned.1.call-done = bf16[384,768]{1,0:T(8,128)(2,1)} async-done(((bf16[3072,768]{1,0:T(8,128)(2,1)}), bf16[384,768]{1,0:T(8,128)(2,1)}) %reduce-scatter.11.cloned.1.call-update) | async-done | bytes 589840 | tf_op jit(solution)/shard_map/reduce_scatter | solution.py:191
  480.0 8.0 %all-gather = s32[1,2048]{1,0:T(1,128)S(1)} all-gather(s32[1,512]{1,0:T(1,128)S(1)} %copy-done.21), channel_id=2, replica_groups=mesh['ctx'=4,'wsh'=8] {'ctx'}, dimensions={1}, use_global_device_ids=true | all-gather | bytes 10240 | tf_op jit(solution)/shard_map/all_gather | solution.py:81
  488.7 37.6 %psum.36 = f32[8,1152]{1,0:T(8,128)S(1)} all-reduce(f32[8,1152]{1,0:T(8,128)S(1)} %concatenate.19), channel_id=1, replica_groups=mesh['ctx'=4,'wsh'=8] {'ctx','wsh'}, use_global_device_ids=true, to_apply=%region_22.23 | all-reduce | flops 9216 | bytes 73728 | tf_op jit(solution)/shard_map/psum | solution.py:208
  527.5 4.9 fusion.22
  532.4 40.1 %all-gather.21.cloned.1.call-done = bf16[2048,768]{1,0:T(8,128)(2,1)} async-done(((bf16[512,768]{1,0:T(8,128)(2,1)}), bf16[2048,768]{1,0:T(8,128)(2,1)}) %all-gather.21.cloned.1.call-update) | async-done | bytes 3145744 | tf_op jit(solution)/shard_map/all_gather | solution.py:135
  572.5 4.6 fusion.32
  577.1 63.9 %all-reduce.3.cloned.1.call-done = (bf16[96,2304]{1,0:T(8,128)(2,1)}, bf16[96,768]{1,0:T(8,128)(2,1)}, bf16[96,3072]{1,0:T(8,128)(2,1)}, bf16[384,768]{1,0:T(8,128)(2,1)}) async-done(((bf16[96,2304]{1,0:T(8,128)(2,1)}, bf16[96,768]{1,0:T(8,128)(2,1)}, bf16[96,3072]{1,0:T(8,128)(2,1)}, bf16[384,768]{1,0:T(8,128)(2,1)}), (bf16[96,2304]{1,0:T(8,128)(2,1)}, bf16[96,768]{1,0:T(8,128)(2,1)}, ...) | async-done | bytes 1769488 | tf_op jit(solution)/shard_map/psum | solution.py:192
  641.0 2.2 convert_element_type.246
  643.3 2.2 convert_element_type.248
  (152 shorter events, 16.5 us)
Async XLA Ops:
  7.2 76.1 %all-gather.11.cloned.1.call-start = ((), (), s32[]{:S(2)}) async-start(), calls=%async_computation.4 | async-start | bytes 7864320 | tf_op jit(solution)/shard_map/all_gather | solution.py:82
  9.8 2.8 copy-start.22
  9.8 2.8 copy-start.23
  9.9 2.8 copy-start.24
  9.9 2.8 copy-start.25
  9.9 2.8 copy-start.26
  9.9 2.8 copy-start.27
  9.9 2.8 copy-start.28
  9.9 2.8 copy-start.29
  9.9 2.8 copy-start.30
  9.9 19.3 %copy-start.21 = (s32[1,512]{1,0:T(1,128)S(1)}, s32[1,512]{1,0:T(1,128)}, u32[]{:S(2)}) copy-start(s32[1,512]{1,0:T(1,128)} %param.17) | copy-start | bytes 6148
  10.0 116.6 %all-gather.13.cloned.1.call-start = ((), (), s32[]{:S(2)}) async-start(), calls=%async_computation.5 | async-start | bytes 3981312 | tf_op jit(solution)/shard_map/all_gather | solution.py:85
  10.7 139.0 %all-gather.15.cloned.1.call-start = ((), (), s32[]{:S(2)}) async-start(), calls=%async_computation.6 | async-start | bytes 1327104 | tf_op jit(solution)/shard_map/all_gather | solution.py:86
  11.4 191.3 %all-gather.17.cloned.1.call-start = ((), (), s32[]{:S(2)}) async-start(), calls=%async_computation.7 | async-start | bytes 5308416 | tf_op jit(solution)/shard_map/all_gather | solution.py:87
  12.0 242.8 %all-gather.19.cloned.1.call-start = ((), (), s32[]{:S(2)}) async-start(), calls=%async_computation.8 | async-start | bytes 5308416 | tf_op jit(solution)/shard_map/all_gather | solution.py:88
  12.6 316.4 %reduce-scatter.7.cloned.1.call-start = ((), (), s32[]{:S(2)}) async-start(), calls=%async_computation.12 | async-start | bytes 1327104 | tf_op jit(solution)/shard_map/reduce_scatter | solution.py:191
  89.2 41.4 %copy-start = (f32[512,1536]{1,0:T(8,128)}, f32[512,1536]{1,0:T(8,128)S(1)}, u32[]{:S(2)}) copy-start(f32[512,1536]{1,0:T(8,128)S(1)} %fusion.12) | copy-start | bytes 9437188
  132.0 1.7 copy-start.9
  133.5 1.2 copy-start.8
  135.1 1.7 copy-start.15
  136.8 1.6 copy-start.11
  139.0 13.4 %copy-start.6 = (bf16[4,128,12,64]{1,0,3,2:T(4,128)(2,1)}, bf16[4,128,12,64]{1,0,3,2:T(4,128)(2,1)S(1)}, u32[]{:S(2)}) copy-start(bf16[4,128,12,64]{1,0,3,2:T(4,128)(2,1)S(1)} %copy.70) | copy-start | bytes 2359300
  152.4 116.5 %copy-start.5 = (bf16[512,768]{1,0:T(8,128)(2,1)}, bf16[512,768]{1,0:T(8,128)(2,1)S(1)}, u32[]{:S(2)}) copy-start(bf16[512,768]{1,0:T(8,128)(2,1)S(1)} %get-tuple-element.54) | copy-start | bytes 2359300
  254.8 7.0 %copy-start.1 = (f32[512,1536]{1,0:T(8,128)S(1)}, f32[512,1536]{1,0:T(8,128)}, u32[]{:S(2)}) copy-start(f32[512,1536]{1,0:T(8,128)} %copy-done) | copy-start | bytes 9437188
  254.8 9.4 %copy-start.33 = (f32[512,3072]{1,0:T(8,128)S(1)}, f32[512,3072]{1,0:T(8,128)}, u32[]{:S(2)}) copy-start(f32[512,3072]{1,0:T(8,128)} %get-tuple-element.56) | copy-start | bytes 18874372
  261.8 2.4 copy-start.31
  262.6 6.3 slice-start
  264.2 4.8 copy-start.13
  264.2 4.8 slice-start.1
  268.9 3.3 copy-start.34
  272.2 1.9 copy-start.32
  274.1 13.5 %copy-start.3 = (f32[512,768]{1,0:T(8,128)}, f32[512,768]{1,0:T(8,128)S(1)}, u32[]{:S(2)}) copy-start(f32[512,768]{1,0:T(8,128)S(1)} %get-tuple-element.30) | copy-start | bytes 4718596
  280.8 4.4 copy-start.12
  280.8 4.4 copy-start.16
  280.8 4.4 copy-start.17
  285.2 2.5 copy-start.7
  292.1 76.1 %reduce-scatter.5.cloned.1.call-start = ((), (), s32[]{:S(2)}) async-start(), calls=%async_computation.11 | async-start | bytes 3981312 | tf_op jit(solution)/shard_map/reduce_scatter | solution.py:191
  299.1 2.7 copy-start.2
  299.7 1.4 copy-start.19
  305.7 118.5 %reduce-scatter.9.cloned.1.call-start = ((), (), s32[]{:S(2)}) async-start(), calls=%async_computation.13 | async-start | bytes 5308416 | tf_op jit(solution)/shard_map/reduce_scatter | solution.py:191
  312.9 1.4 copy-start.14
  313.0 167.0 %reduce-scatter.11.cloned.1.call-start = ((), (), s32[]{:S(2)}) async-start(), calls=%async_computation.14 | async-start | bytes 5308416 | tf_op jit(solution)/shard_map/reduce_scatter | solution.py:191
  321.1 1.4 copy-start.4
  321.1 206.4 %all-gather.23.cloned.1.call-start = ((), (), s32[]{:S(2)}) async-start(), calls=%async_computation.10 | async-start | bytes 3932160 | tf_op jit(solution)/shard_map/all_gather | solution.py:187
  328.2 244.4 %all-gather.21.cloned.1.call-start = ((), (), s32[]{:S(2)}) async-start(), calls=%async_computation.9 | async-start | bytes 3932160 | tf_op jit(solution)/shard_map/all_gather | solution.py:135
  328.9 312.1 %all-reduce.3.cloned.1.call-start = ((), (), s32[]{:S(2)}) async-start(), calls=%async_computation.15 | async-start | bytes 3538944 | tf_op jit(solution)/shard_map/psum | solution.py:192
  641.0 4.4 copy-start.18
  641.0 5.4 copy-start.20
  (1 other events, 1.1 us)
Sparse Core Ops, SparseCore 0:
  10.4 72.8 all-gather.10
  85.0 41.5 all-gather.12
  128.2 21.5 all-gather.14
  151.2 51.4 all-gather.16
  204.2 50.5 all-gather.18
  292.2 31.5 reduce-scatter.6
  326.2 42.0 reduce-scatter.4
  370.7 53.4 reduce-scatter.8
  426.6 53.3 reduce-scatter.10
  482.3 43.4 all-gather.22
  528.4 44.0 all-gather.20
  576.2 64.7 all-reduce.2
where the time goes:
time: 663 us; the launch traced here: 654 us
  waiting for transfers between devices  451 us (68%)
  matrix products  82.5 us (12%)
  blocking collectives  61.3 us (9%)
  local copies, waits for them, and re-layouts  22.8 us (3%)
  other arithmetic  20.3 us (3%)
  between operations  15.1 us (2%)
    reduce_scatter x4, waiting for transfers between devices, summed(): part = lax.psum_scatter(grad, 'wsh', scatter_dimension=0, tiled=True)  151 us
    psum x1, waiting for transfers between devices, summed(): return lax.psum(part, 'ctx').astype(jnp.float32)  63.9 us
    all_gather x1, waiting for transfers between devices, on_device(): lax.all_gather(jnp.concatenate([tokens[0], cotangent[0]], axis=1), 'ctx',...  53.9 us
    all_gather x1, waiting for transfers between devices, on_device(): whole_up = lax.all_gather(up_weight, 'wsh', axis=0, tiled=True)  48.2 us
    all_gather x1, waiting for transfers between devices, on_device(): whole_down = lax.all_gather(down_weight, 'wsh', axis=0, tiled=True)  43 us
    all_gather x1, waiting for transfers between devices, on_device(): group_out = lax.all_gather(layer_out, 'ctx', axis=0, tiled=True)  40.1 us
    psum x1, blocking collectives, on_device(): table = lax.psum(table, ('ctx', 'wsh'))  37.6 us
    all_gather x1, waiting for transfers between devices, on_device(): whole_qkv = lax.all_gather(qkv_weight, 'wsh', axis=0, tiled=True)  37.4 us
  transfers between devices with their start and end apart: 12, of which 10 were waited for; matrix products, arithmetic and copies ran while one was open for 11% of the time, Pallas kernels for 0%

commit v1 on v0

--- a/solution.py
+++ b/solution.py
@@ -6,6 +6,11 @@
 HEAD_DIM = 64
 CLUSTER = 128
 epsilon = 1e-05
+
+
+def gather_and_add(x, axis):
+    parts = lax.all_gather(x, axis)
+    return jnp.sum(parts, axis=0)
 
 
 def inner(left, right):
@@ -189,7 +194,7 @@
 
     def summed(grad):
         part = lax.psum_scatter(grad, "wsh", scatter_dimension=0, tiled=True)
-        return lax.psum(part, "ctx").astype(jnp.float32)
+        return gather_and_add(part, "ctx").astype(jnp.float32)
 
     sums = [summed(g) for g in (grad_down_w, grad_up_w, grad_out_w, grad_qkv_w)]
     small_grads = [

time: 663 us -> 706 us (1.065)
  waiting for transfers between devices: 451 us -> 479 us
  blocking collectives: 61.3 us -> 73.9 us
  matrix products: 82.5 us -> 90.1 us
    all_gather x0 -> x3, waiting for transfers between devices: none -> 103 us  [gather_and_add(): parts = lax.all_gather(x, axis)]
    psum x1 -> x0, waiting for transfers between devices: 63.9 us -> none  [summed(): return lax.psum(part, 'ctx').astype(jnp.float32)]
    reduce_scatter x4, waiting for transfers between devices: 151 us -> 129 us  [summed(): part = lax.psum_scatter(grad, 'wsh', scatter_dimension=0, tiled=True)]
    all_gather x1, waiting for transfers between devices: 0.01 us -> 19.8 us  [on_device(): group_in = lax.all_gather(grad_inputs, 'ctx', axis=0, tiled=True)]
    all_gather x0 -> x1, blocking collectives: none -> 12.7 us  [gather_and_add(): parts = lax.all_gather(x, axis)]
    dot_general x1, matrix products: 9.02 us -> 20 us  [on_device(): jnp.dot(first_low, whole_up, preferred_element_type=jnp.float32) + ubias]
    all_gather x1, waiting for transfers between devices: 43 us -> 32 us  [on_device(): whole_down = lax.all_gather(down_weight, 'wsh', axis=0, tiled=True)]
  transfers between devices with their start and end apart: 12 -> 14, of which waited for: 10 -> 13; matrix products, arithmetic and copies ran while one was open for 11% -> 12% of each run, Pallas kernels for 0% -> 0%
where the time goes in v1:
time: 706 us; the launch traced here: 697 us
  waiting for transfers between devices  479 us (68%)
  matrix products  90.1 us (13%)
  blocking collectives  73.9 us (10%)
  other arithmetic  20.4 us (3%)
  local copies, waits for them, and re-layouts  18 us (3%)
  between operations  15 us (2%)
    reduce_scatter x4, waiting for transfers between devices, summed(): part = lax.psum_scatter(grad, 'wsh', scatter_dimension=0, tiled=True)  129 us
    all_gather x3, waiting for transfers between devices, gather_and_add(): parts = lax.all_gather(x, axis)  103 us
    all_gather x1, waiting for transfers between devices, on_device(): lax.all_gather(jnp.concatenate([tokens[0], cotangent[0]], axis=1), 'ctx',...  53.9 us
    all_gather x1, waiting for transfers between devices, on_device(): whole_up = lax.all_gather(up_weight, 'wsh', axis=0, tiled=True)  48.2 us
    all_gather x1, waiting for transfers between devices, on_device(): group_out = lax.all_gather(layer_out, 'ctx', axis=0, tiled=True)  41.7 us
    psum x1, blocking collectives, on_device(): table = lax.psum(table, ('ctx', 'wsh'))  37.5 us
    all_gather x1, waiting for transfers between devices, on_device(): whole_qkv = lax.all_gather(qkv_weight, 'wsh', axis=0, tiled=True)  37.4 us
    all_gather x1, waiting for transfers between devices, on_device(): whole_down = lax.all_gather(down_weight, 'wsh', axis=0, tiled=True)  32 us
  transfers between devices with their start and end apart: 14, of which 13 were waited for; matrix products, arithmetic and copies ran while one was open for 12% of the time, Pallas kernels for 0%

profile of v1, /device:TPU:0, one launch (start us, length us, event | category | flops | bytes accessed | tf_op | source)
XLA Modules:
  0.0 696.8 jit_solution(15674654837465826455)
XLA Ops:
  7.2 2.6 pad_maximum_fusion
  12.8 15.7 %all-gather.6 = bf16[8,1,1152]{2,1,0:T(2,128)(2,1)S(1)} all-gather(bf16[1,1,1152]{2,1,0:T(2,128)(2,1)S(1)} %reshape.241), channel_id=3, replica_groups=mesh['ctx'=4,'wsh'=8] {'wsh'}, dimensions={0}, use_global_device_ids=true | all-gather | bytes 20736 | tf_op jit(solution)/shard_map/all_gather | solution.py:81
  29.4 53.9 %all-gather.18.cloned.1.call-done = bf16[2048,1536]{1,0:T(8,128)(2,1)} async-done(((bf16[512,1536]{1,0:T(8,128)(2,1)}), bf16[2048,1536]{1,0:T(8,128)(2,1)}) %all-gather.18.cloned.1.call-update) | async-done | bytes 6291472 | tf_op jit(solution)/shard_map/all_gather | solution.py:87
  83.3 5.8 fusion.12
  89.2 37.4 %all-gather.20.cloned.1.call-done = bf16[768,2304]{1,0:T(8,128)(2,1)} async-done(((bf16[96,2304]{1,0:T(8,128)(2,1)}), bf16[768,2304]{1,0:T(8,128)(2,1)}) %all-gather.20.cloned.1.call-update) | async-done | bytes 3538960 | tf_op jit(solution)/shard_map/all_gather | solution.py:90
  126.5 4.0 fusion.11
  130.5 1.4 fusion.67
  132.0 1.5 copy.64
  137.4 1.1 copy-done.10
  139.1 10.7 %all-gather.22.cloned.1.call-done = bf16[768,768]{1,0:T(8,128)(2,1)} async-done(((bf16[96,768]{1,0:T(8,128)(2,1)}), bf16[768,768]{1,0:T(8,128)(2,1)}) %all-gather.22.cloned.1.call-update) | async-done | bytes 1179664 | tf_op jit(solution)/shard_map/all_gather | solution.py:91
  149.7 2.7 fusion.26
  152.4 2.1 multiply_reduce_fusion.6
  154.5 48.2 %all-gather.24.cloned.1.call-done = bf16[768,3072]{1,0:T(8,128)(2,1)} async-done(((bf16[96,3072]{1,0:T(8,128)(2,1)}), bf16[768,3072]{1,0:T(8,128)(2,1)}) %all-gather.24.cloned.1.call-update) | async-done | bytes 4718608 | tf_op jit(solution)/shard_map/all_gather | solution.py:92
  202.8 20.0 %multiply_convert_fusion = (bf16[512,3072]{1,0:T(8,128)(2,1)}, f32[512,3072]{1,0:T(8,128)}) fusion(f32[3072]{0:T(1024)S(1)} %reshape.231, bf16[768,3072]{1,0:T(8,128)(2,1)} %all-gather.24.cloned.1.call-done, f32[768]{0:T(1024)S(1)} %reshape.230, f32[768]{0:T(1024)S(1)} %reshape.229, f32[512]{0:T(512)S(1)} %add_rsqrt_fusion.1, ...), kind=kOutput, calls=%fused_computation.9 | convolution fusion | flops 2428502016 | bytes 15751168 | tf_op jit(solution)/shard_map/dot_general | solution.py:133
  222.8 32.0 %all-gather.26.cloned.1.call-done = bf16[3072,768]{1,0:T(8,128)(2,1)} async-done(((bf16[384,768]{1,0:T(8,128)(2,1)}), bf16[3072,768]{1,0:T(8,128)(2,1)}) %all-gather.26.cloned.1.call-update) | async-done | bytes 4718608 | tf_op jit(solution)/shard_map/all_gather | solution.py:93
  254.8 6.7 fusion.69
  262.7 1.5 convert_reduce_fusion.1
  264.2 4.7 convert_reduce_fusion
  269.0 3.2 multiply_reduce_fusion.2
  272.9 1.1 copy-done.3
  275.4 3.3 convert_reduce_fusion.3
  281.3 1.2 fusion.38
  284.7 1.4 copy-done.16
  287.1 4.1 convolution_convert_fusion.2
  291.2 7.2 %convolution_convert_fusion.1 = bf16[768,3072]{1,0:T(8,128)(2,1)} fusion(bf16[512,3072]{1,0:T(8,128)(2,1)} %copy-done.30, f32[768]{0:T(1024)S(1)} %reshape.230, f32[768]{0:T(1024)S(1)} %reshape.229, bf16[512,768]{1,0:T(8,128)(2,1)} %copy-done.7, f32[512]{0:T(512)S(1)} %add_rsqrt_fusion.1, f32[512]{0:T(512)S(1)} %broadcast_multiply_fusion.5, ...), kind=kOutput, calls=%fused_computation.16 | convolution fusion | flops 2421424128 | bytes 9449472 | tf_op jit(solution)/shard_map/dot_general | solution.py:17
  298.5 1.3 copy-done.13
  299.8 6.7 convolution_convert_fusion
  306.6 1.3 copy-done.4
  308.1 1.8 convolution_convert_fusion.3
  310.0 5.7 add_convert_fusion
  316.5 17.5 %reduce-scatter.5.cloned.1.call-done = bf16[96,2304]{1,0:T(8,128)(2,1)} async-done(((bf16[768,2304]{1,0:T(8,128)(2,1)}), bf16[96,2304]{1,0:T(8,128)(2,1)}) %reduce-scatter.5.cloned.1.call-update) | async-done | bytes 442384 | tf_op jit(solution)/shard_map/reduce_scatter | solution.py:196
  334.0 55.9 %reduce-scatter.9.cloned.1.call-done = bf16[96,3072]{1,0:T(8,128)(2,1)} async-done(((bf16[768,3072]{1,0:T(8,128)(2,1)}), bf16[96,3072]{1,0:T(8,128)(2,1)}) %reduce-scatter.9.cloned.1.call-update) | async-done | bytes 589840 | tf_op jit(solution)/shard_map/reduce_scatter | solution.py:196
  389.9 55.7 %reduce-scatter.11.cloned.1.call-done = bf16[384,768]{1,0:T(8,128)(2,1)} async-done(((bf16[3072,768]{1,0:T(8,128)(2,1)}), bf16[384,768]{1,0:T(8,128)(2,1)}) %reduce-scatter.11.cloned.1.call-update) | async-done | bytes 589840 | tf_op jit(solution)/shard_map/reduce_scatter | solution.py:196
  445.7 8.0 %all-gather = s32[1,2048]{1,0:T(1,128)S(1)} all-gather(s32[1,512]{1,0:T(1,128)S(1)} %copy-done.17), channel_id=2, replica_groups=mesh['ctx'=4,'wsh'=8] {'ctx'}, dimensions={1}, use_global_device_ids=true | all-gather | bytes 10240 | tf_op jit(solution)/shard_map/all_gather | solution.py:86
  454.4 37.5 %psum.7 = f32[8,1152]{1,0:T(8,128)S(1)} all-reduce(f32[8,1152]{1,0:T(8,128)S(1)} %concatenate.19), channel_id=1, replica_groups=mesh['ctx'=4,'wsh'=8] {'ctx','wsh'}, use_global_device_ids=true, to_apply=%region_22.23 | all-reduce | flops 9216 | bytes 73728 | tf_op jit(solution)/shard_map/psum | solution.py:213
  493.2 12.7 %all-gather.3 = bf16[384,768]{1,0:T(8,128)(2,1)S(1)} all-gather(bf16[96,768]{1,0:T(8,128)(2,1)} %reduce-scatter.7.cloned.1.call-done), channel_id=5, replica_groups=mesh['ctx'=4,'wsh'=8] {'ctx'}, dimensions={0}, use_global_device_ids=true | all-gather | bytes 737280 | tf_op jit(solution)/shard_map/all_gather | solution.py:12
  506.7 19.8 %all-gather.30.cloned.1.call-done = bf16[2048,768]{1,0:T(8,128)(2,1)} async-done(((bf16[512,768]{1,0:T(8,128)(2,1)}), bf16[2048,768]{1,0:T(8,128)(2,1)}) %all-gather.30.cloned.1.call-update) | async-done | bytes 3145744 | tf_op jit(solution)/shard_map/all_gather | solution.py:192
  526.5 4.9 fusion.22
  531.4 41.7 %all-gather.28.cloned.1.call-done = bf16[2048,768]{1,0:T(8,128)(2,1)} async-done(((bf16[512,768]{1,0:T(8,128)(2,1)}), bf16[2048,768]{1,0:T(8,128)(2,1)}) %all-gather.28.cloned.1.call-update) | async-done | bytes 3145744 | tf_op jit(solution)/shard_map/all_gather | solution.py:140
  573.1 4.6 fusion.32
  577.7 29.9 %all-gather.32.cloned.1.call-done = bf16[384,2304]{1,0:T(8,128)(2,1)} async-done(((bf16[96,2304]{1,0:T(8,128)(2,1)}), bf16[384,2304]{1,0:T(8,128)(2,1)}) %all-gather.32.cloned.1.call-update) | async-done | bytes 1769488 | tf_op jit(solution)/shard_map/all_gather | solution.py:12
  607.6 1.8 reduce_sum.229
  610.3 36.7 %all-gather.34.cloned.1.call-done = bf16[384,3072]{1,0:T(8,128)(2,1)} async-done(((bf16[96,3072]{1,0:T(8,128)(2,1)}), bf16[384,3072]{1,0:T(8,128)(2,1)}) %all-gather.34.cloned.1.call-update) | async-done | bytes 2359312 | tf_op jit(solution)/shard_map/all_gather | solution.py:12
  647.1 2.1 reduce_sum.240
  649.2 1.1 convert_element_type.254
  650.3 36.1 %all-gather.36.cloned.1.call-done = bf16[1536,768]{1,0:T(8,128)(2,1)} async-done(((bf16[384,768]{1,0:T(8,128)(2,1)}), bf16[1536,768]{1,0:T(8,128)(2,1)}) %all-gather.36.cloned.1.call-update) | async-done | bytes 2359312 | tf_op jit(solution)/shard_map/all_gather | solution.py:12
  686.4 2.3 reduce_sum.241
  688.7 1.1 convert_element_type.256
  (155 shorter events, 22.0 us)
Async XLA Ops:
  7.2 76.1 %all-gather.18.cloned.1.call-start = ((), (), s32[]{:S(2)}) async-start(), calls=%async_computation.4 | async-start | bytes 7864320 | tf_op jit(solution)/shard_map/all_gather | solution.py:87
  9.8 2.8 copy-start.18
  9.9 2.8 copy-start.19
  9.9 2.8 copy-start.20
  9.9 2.8 copy-start.21
  9.9 2.8 copy-start.22
  9.9 2.8 copy-start.23
  9.9 2.8 copy-start.24
  9.9 2.8 copy-start.25
  9.9 2.8 copy-start.26
  9.9 19.3 %copy-start.17 = (s32[1,512]{1,0:T(1,128)S(1)}, s32[1,512]{1,0:T(1,128)}, u32[]{:S(2)}) copy-start(s32[1,512]{1,0:T(1,128)} %param.17) | copy-start | bytes 6148
  10.0 116.6 %all-gather.20.cloned.1.call-start = ((), (), s32[]{:S(2)}) async-start(), calls=%async_computation.5 | async-start | bytes 3981312 | tf_op jit(solution)/shard_map/all_gather | solution.py:90
  10.7 139.0 %all-gather.22.cloned.1.call-start = ((), (), s32[]{:S(2)}) async-start(), calls=%async_computation.6 | async-start | bytes 1327104 | tf_op jit(solution)/shard_map/all_gather | solution.py:91
  11.4 191.3 %all-gather.24.cloned.1.call-start = ((), (), s32[]{:S(2)}) async-start(), calls=%async_computation.7 | async-start | bytes 5308416 | tf_op jit(solution)/shard_map/all_gather | solution.py:92
  12.0 242.8 %all-gather.26.cloned.1.call-start = ((), (), s32[]{:S(2)}) async-start(), calls=%async_computation.8 | async-start | bytes 5308416 | tf_op jit(solution)/shard_map/all_gather | solution.py:93
  12.6 321.3 %reduce-scatter.5.cloned.1.call-start = ((), (), s32[]{:S(2)}) async-start(), calls=%async_computation.11 | async-start | bytes 3981312 | tf_op jit(solution)/shard_map/reduce_scatter | solution.py:196
  89.2 41.4 %copy-start = (f32[512,1536]{1,0:T(8,128)}, f32[512,1536]{1,0:T(8,128)S(1)}, u32[]{:S(2)}) copy-start(f32[512,1536]{1,0:T(8,128)S(1)} %fusion.12) | copy-start | bytes 9437188
  132.0 1.7 copy-start.9
  133.5 1.2 copy-start.8
  135.1 1.7 copy-start.14
  136.8 1.7 copy-start.10
  139.1 13.3 %copy-start.5 = (bf16[4,128,12,64]{1,0,3,2:T(4,128)(2,1)}, bf16[4,128,12,64]{1,0,3,2:T(4,128)(2,1)S(1)}, u32[]{:S(2)}) copy-start(bf16[4,128,12,64]{1,0,3,2:T(4,128)(2,1)S(1)} %copy.70) | copy-start | bytes 2359300
  152.4 119.8 %copy-start.7 = (bf16[512,768]{1,0:T(8,128)(2,1)}, bf16[512,768]{1,0:T(8,128)(2,1)S(1)}, u32[]{:S(2)}) copy-start(bf16[512,768]{1,0:T(8,128)(2,1)S(1)} %get-tuple-element.50) | copy-start | bytes 2359300
  254.8 7.0 %copy-start.1 = (f32[512,1536]{1,0:T(8,128)S(1)}, f32[512,1536]{1,0:T(8,128)}, u32[]{:S(2)}) copy-start(f32[512,1536]{1,0:T(8,128)} %copy-done) | copy-start | bytes 9437188
  254.8 9.4 %copy-start.29 = (f32[512,3072]{1,0:T(8,128)S(1)}, f32[512,3072]{1,0:T(8,128)}, u32[]{:S(2)}) copy-start(f32[512,3072]{1,0:T(8,128)} %get-tuple-element.52) | copy-start | bytes 18874372
  261.8 2.4 copy-start.27
  262.7 6.3 slice-start
  264.2 4.8 copy-start.12
  264.2 4.8 slice-start.1
  268.9 3.3 copy-start.30
  272.3 1.8 copy-start.28
  272.9 1.1 copy-start.3
  275.3 3.4 copy-start.11
  275.4 3.4 copy-start.15
  284.3 2.7 copy-start.2
  284.7 1.4 copy-start.16
  291.2 98.7 %reduce-scatter.9.cloned.1.call-start = ((), (), s32[]{:S(2)}) async-start(), calls=%async_computation.13 | async-start | bytes 5308416 | tf_op jit(solution)/shard_map/reduce_scatter | solution.py:196
  298.4 1.4 copy-start.13
  298.4 147.2 %reduce-scatter.11.cloned.1.call-start = ((), (), s32[]{:S(2)}) async-start(), calls=%async_computation.14 | async-start | bytes 5308416 | tf_op jit(solution)/shard_map/reduce_scatter | solution.py:196
  306.5 1.4 copy-start.4
  306.5 1.6 copy-start.6
  306.5 186.6 %reduce-scatter.7.cloned.1.call-start = ((), (), s32[]{:S(2)}) async-start(), calls=%async_computation.12 | async-start | bytes 1327104 | tf_op jit(solution)/shard_map/reduce_scatter | solution.py:196
  309.9 216.6 %all-gather.30.cloned.1.call-start = ((), (), s32[]{:S(2)}) async-start(), calls=%async_computation.10 | async-start | bytes 3932160 | tf_op jit(solution)/shard_map/all_gather | solution.py:192
  315.7 257.4 %all-gather.28.cloned.1.call-start = ((), (), s32[]{:S(2)}) async-start(), calls=%async_computation.9 | async-start | bytes 3932160 | tf_op jit(solution)/shard_map/all_gather | solution.py:140
  316.4 291.1 %all-gather.32.cloned.1.call-start = ((), (), s32[]{:S(2)}) async-start(), calls=%async_computation.15 | async-start | bytes 2211840 | tf_op jit(solution)/shard_map/all_gather | solution.py:12
  334.0 313.1 %all-gather.34.cloned.1.call-start = ((), (), s32[]{:S(2)}) async-start(), calls=%async_computation.16 | async-start | bytes 2949120 | tf_op jit(solution)/shard_map/all_gather | solution.py:12
  389.9 296.5 %all-gather.36.cloned.1.call-start = ((), (), s32[]{:S(2)}) async-start(), calls=%async_computation.17 | async-start | bytes 2949120 | tf_op jit(solution)/shard_map/all_gather | solution.py:12
Sparse Core Ops, SparseCore 0:
  10.4 72.8 all-gather.17
  85.0 41.5 all-gather.19
  128.2 21.5 all-gather.21
  151.2 51.4 all-gather.23
  204.2 50.5 all-gather.25
  291.3 42.6 reduce-scatter.4
  336.4 53.4 reduce-scatter.8
  392.3 53.3 reduce-scatter.10
  448.6 31.4 reduce-scatter.6
  482.5 43.9 all-gather.29
  529.1 43.9 all-gather.27
  574.9 32.5 all-gather.31
  609.5 37.4 all-gather.33
  648.9 37.4 all-gather.35
